TPU v7x, 32 devices: a whole 2x2x4 slice. The times are simulated.
32 devices in a mesh: gx: 4 (over x, core), gy: 8 (over z, y).
Axes of the slice: x: 2, y: 2, z: 4, core: 2. Of those that a mesh axis runs over, the one named last changes fastest.
Arguments:
- primal_pops: float32 [27, 64, 64, 6], P(None, 'gx', 'gy'), may hold values from 0.2 to 1.8
- tangent_pops: float32 [27, 64, 64, 384], P(None, 'gx', 'gy'), may hold values from -6 to 6
- inflow_pops: float32 [9, 64, 6], replicated, may hold values from 0.2 to 1.8
- inflow_sens: float32 [9, 64, 384], replicated, may hold values from -6 to 6
- w_in: float32 [128, 27], replicated, may hold values from -1.25 to 1.25
- b_in: float32 [128], replicated, may hold values from -3 to 3
- w_mid: float32 [128, 128], replicated, may hold values from -0.5 to 0.5
- b_mid: float32 [128], replicated, may hold values from -3 to 3
- w_out: float32 [27, 128], replicated, may hold values from -0.5 to 0.5
- b_out: float32 [27], replicated, may hold values from -2 to 2
- probe_cells: int32 [32, 32, 4], P(('gx', 'gy')), may hold values from 0 to 767
- probe_counts: int32 [32, 32], P(('gx', 'gy')), may hold values from 0 to 4, as said below
Outputs:
- primal_out: float32 [27, 64, 64, 6], P(None, 'gx', 'gy')
- tangent_out: float32 [27, 64, 64, 384], P(None, 'gx', 'gy')
- jac_rows: float32 [32, 32, 4, 256], P(('gx', 'gy'))
Inputs may be any that keep to these rules, and one draw needn't show every extreme that they name: `probe_cells`: a local cell of the holder; slots at or beyond probe_counts for that owner are unused. `probe_counts`: in every draw one owner receives exactly 4 probes from every holder.
All inputs are finite; a program needn't handle non-finite values.
Results may differ from a plain program's by a relative error of at most 0.00011.
Values sent between devices are 32-bit elements; how exact they have to be, the bound alone decides.
A program may use at most 128 MiB of HBM per device.

v0:
```python
import functools

import jax
import jax.numpy as jnp
from jax import lax
from jax.experimental import pallas as pl
from jax.experimental.pallas import tpu as pltpu
from jax.sharding import PartitionSpec as P

STEPS = 2
QS = 32
LANES = 128
GROUP = 6
VMEM_LIMIT = 60 * 1024 * 1024
LATTICE = [(q // 9 - 1, q // 3 % 3 - 1, q % 3 - 1) for q in range(27)]
precise = lax.Precision.HIGHEST


def split(value):
    high = value.astype(jnp.bfloat16)
    low = (value - high.astype(jnp.float32)).astype(jnp.bfloat16)
    return high, low


def dot(a, b):
    return jnp.dot(a, b, preferred_element_type=jnp.float32)


def lane_iota(rows):
    return lax.broadcasted_iota(jnp.int32, (rows, LANES), 1)


def primal_collide(state_ref, weights, post_ref, slope_one_ref, slope_two_ref):
    w_in, b_in, w_mid, b_mid, w_out, b_out = weights
    rows_x = post_ref.shape[1]

    def one(x, carry):
        cell = state_ref[pl.ds(x, QS, stride=rows_x), :]
        first = jnp.dot(w_in[...], cell, precision=precise, preferred_element_type=jnp.float32)
        act_one = jnp.tanh(first + b_in[...])
        second = jnp.dot(w_mid[...], act_one, precision=precise, preferred_element_type=jnp.float32)
        act_two = jnp.tanh(second + b_mid[...])
        moved = jnp.dot(w_out[...], act_two, precision=precise, preferred_element_type=jnp.float32)
        slope_one_ref[x] = 1.0 - act_one * act_one
        slope_two_ref[x] = 1.0 - act_two * act_two
        state_ref[pl.ds(x, QS, stride=rows_x), :] = cell + moved + b_out[...]
        return carry

    lax.fori_loop(0, rows_x, one, 0)
    for q in range(27):
        post_ref[q] = state_ref[q * rows_x : (q + 1) * rows_x, :]


def primal_stream(post_ref, x_low, x_high, y_low, y_high, write, z_depth):
    rows_x, rows_y = post_ref.shape[1], 8
    lane = lane_iota(rows_x)
    at_y = lane % rows_y
    last_z = (z_depth - 1) * rows_y
    for q, (ex, ey, ez) in enumerate(LATTICE):
        own = post_ref[q]
        if ex == 1:
            own = jnp.concatenate([x_low[q - 18], own[: rows_x - 1]], axis=0)
        elif ex == -1:
            own = jnp.concatenate([own[1:], x_high[q]], axis=0)
        if ey != 0:
            j = (ex + 1) * 3 + ez + 1
            side = (y_low if ey == 1 else y_high)[j, 1 - ex : 1 - ex + rows_x]
            if ey == 1:
                own = jnp.where(at_y == 0, pltpu.roll(side, LANES - rows_y + 1, 1), pltpu.roll(own, 1, 1))
            else:
                own = jnp.where(at_y == rows_y - 1, pltpu.roll(side, rows_y - 1, 1), pltpu.roll(own, LANES - 1, 1))
        if ez == 1:
            own = jnp.where(lane < rows_y, post_ref[26 - q], pltpu.roll(own, rows_y, 1))
        elif ez == -1:
            own = jnp.where(lane >= last_z, post_ref[26 - q], pltpu.roll(own, LANES - rows_y, 1))
        write(q, own)


def primal_first(cells, w_in, b_in, w_mid, b_mid, w_out, b_out, post, slope_one, slope_two, state):
    rows_x = cells.shape[1]
    state[...] = jnp.zeros_like(state)
    for q in range(27):
        state[q * rows_x : (q + 1) * rows_x, :] = cells[q]
    primal_collide(state, (w_in, b_in, w_mid, b_mid, w_out, b_out), post, slope_one, slope_two)


def primal_next(z_depth, before, x_low, x_high, y_low, y_high, w_in, b_in, w_mid, b_mid, w_out, b_out,
                post, slope_one, slope_two, state):
    rows_x = before.shape[1]
    state[...] = jnp.zeros_like(state)

    def write(q, value):
        state[q * rows_x : (q + 1) * rows_x, :] = value

    primal_stream(before, x_low, x_high, y_low, y_high, write, z_depth)
    primal_collide(state, (w_in, b_in, w_mid, b_mid, w_out, b_out), post, slope_one, slope_two)


def primal_last(z_depth, before, x_low, x_high, y_low, y_high, out):
    def write(q, value):
        out[q] = value

    primal_stream(before, x_low, x_high, y_low, y_high, write, z_depth)


def make_weights(w_in, w_mid, w_out, one, two, three):
    high, low = split(w_in[...])
    one[...] = jnp.concatenate([high, high, low], axis=1)
    high, low = split(w_mid[...])
    two[...] = jnp.concatenate(
        [jnp.concatenate([high, high], axis=1), jnp.concatenate([low, jnp.zeros_like(low)], axis=1)], axis=0
    )
    high, low = split(w_out[...])
    three[...] = jnp.concatenate(
        [jnp.concatenate([high, high], axis=1), jnp.concatenate([low, jnp.zeros_like(low)], axis=1)], axis=0
    )


def tangent_collide(state, post, faces, slope_one, slope_two, one, two, three):
    rows_x, pairs = state.shape[0], state.shape[1]
    rows_y = 8
    hidden = two.shape[0] // 2
    below, above, side_low, side_high = faces

    def row(x, carry):
        half = lane_iota(hidden) < LANES // 2
        s_one, s_two = slope_one[x], slope_two[x]

        def scale(slopes, y, pair):
            left = slopes[:, 2 * pair * rows_y + y : 2 * pair * rows_y + y + 1]
            right = slopes[:, (2 * pair + 1) * rows_y + y : (2 * pair + 1) * rows_y + y + 1]
            return jnp.where(half, left, right)

        columns = [(y, pair) for y in range(rows_y) for pair in range(pairs)]
        for start in range(0, len(columns), GROUP):
            here = columns[start : start + GROUP]
            cell = jnp.concatenate([state[x, pair, pl.ds(y, QS, stride=rows_y), :] for y, pair in here], axis=1)
            high, low = split(cell)
            lifted = dot(one[...], jnp.concatenate([high, low, high], axis=0))
            high, low = split(lifted * jnp.concatenate([scale(s_one, y, pair) for y, pair in here], axis=1))
            mixed = dot(two[...], jnp.concatenate([high, low], axis=0))
            mixed = mixed[:hidden] + mixed[hidden:]
            high, low = split(mixed * jnp.concatenate([scale(s_two, y, pair) for y, pair in here], axis=1))
            moved = dot(three[...], jnp.concatenate([high, low], axis=0))
            result = cell + moved[:QS] + moved[QS:]
            for i, (y, pair) in enumerate(here):
                post[x, pair, pl.ds(y, QS, stride=rows_y), :] = result[:, i * LANES : (i + 1) * LANES]
        return carry

    lax.fori_loop(0, rows_x, row, 0)
    stride = pairs * QS * rows_y
    flat = post.reshape(rows_x * stride, LANES)
    for pair in range(pairs):
        lanes = slice(pair * LANES, (pair + 1) * LANES)
        for ex in range(3):
            for ez in range(3):
                q = ex * 9 + 6 + ez
                side_high[ex * 3 + ez, :, lanes] = flat[pl.ds((pair * QS + q + 1) * rows_y - 1, rows_x, stride=stride), :]
                q = ex * 9 + ez
                side_low[ex * 3 + ez, :, lanes] = flat[pl.ds((pair * QS + q) * rows_y, rows_x, stride=stride), :]
        for j in range(9):
            below[j, :, lanes] = post[0, pair, j * rows_y : (j + 1) * rows_y, :]
            above[j, :, lanes] = post[rows_x - 1, pair, (18 + j) * rows_y : (19 + j) * rows_y, :]


def stream_rows(before, x_low, x_high, y_low, y_high, sides, write):
    rows_x, pairs = before.shape[0], before.shape[1]
    rows_y = 8
    lane = lane_iota(rows_y)
    left = lane < LANES // 2
    at_y = lax.broadcasted_iota(jnp.int32, (rows_y, LANES), 0)
    for way, given in enumerate((y_low, y_high)):
        for j in range(9):
            for pair in range(pairs):
                sides[way, j, pair, : rows_x + 2] = given[j, :, pair * LANES : (pair + 1) * LANES]

    def one_row(x, edge):
        for q, (ex, ey, ez) in enumerate(LATTICE):
            parts = []
            for pair in range(pairs):
                lanes = slice(pair * LANES, (pair + 1) * LANES)
                if edge == -1 and ex == 1:
                    value = x_low[q - 18, :, lanes]
                elif edge == 1 and ex == -1:
                    value = x_high[q, :, lanes]
                else:
                    value = before[x - ex, pair, q * rows_y : (q + 1) * rows_y, :]
                if ey != 0:
                    j = (ex + 1) * 3 + ez + 1
                    side = sides[0 if ey == 1 else 1, j, pair, pl.ds(x - ex + 1, 1), :]
                    if ey == 1:
                        value = jnp.where(at_y == 0, side, pltpu.roll(value, 1, 0))
                    else:
                        value = jnp.where(at_y == rows_y - 1, side, pltpu.roll(value, rows_y - 1, 0))
                parts.append(value)
            if ez != 0:
                turned = [pltpu.roll(part, LANES // 2, 1) for part in parts]
                mirror = 26 - q
                if ez == 1:
                    wall = before[x, 0, mirror * rows_y : (mirror + 1) * rows_y, :]
                    parts = [jnp.where(left, turned[p - 1] if p else wall, turned[p]) for p in range(pairs)]
                else:
                    wall = before[x, pairs - 1, mirror * rows_y : (mirror + 1) * rows_y, :]
                    parts = [jnp.where(left, turned[p], turned[p + 1] if p + 1 < pairs else wall) for p in range(pairs)]
            write(x, q, parts)

    one_row(0, -1)

    def inner(x, carry):
        one_row(x, 0)
        return carry

    lax.fori_loop(1, rows_x - 1, inner, 0)
    one_row(rows_x - 1, 1)


def tangent_first(cells, slope_one, slope_two, w_in, w_mid, w_out, post, below, above, side_low, side_high,
                  state, one, two, three):
    rows_x, pairs = state.shape[0], state.shape[1]
    make_weights(w_in, w_mid, w_out, one, two, three)

    def load(x, carry):
        for pair in range(pairs):
            for q in range(27):
                state[x, pair, q * 8 : (q + 1) * 8, :] = cells[q, x, :, pair * LANES : (pair + 1) * LANES]
            state[x, pair, 27 * 8 :, :] = jnp.zeros((5 * 8, LANES), jnp.float32)
        return carry

    lax.fori_loop(0, rows_x, load, 0)
    tangent_collide(state, post, (below, above, side_low, side_high), slope_one, slope_two, one, two, three)


def tangent_next(before, x_low, x_high, y_low, y_high, slope_one, slope_two, w_in, w_mid, w_out,
                 post, below, above, side_low, side_high, state, one, two, three, sides):
    rows_x, pairs = state.shape[0], state.shape[1]
    make_weights(w_in, w_mid, w_out, one, two, three)

    def write(x, q, parts):
        for pair in range(pairs):
            state[x, pair, q * 8 : (q + 1) * 8, :] = parts[pair]
            if q == 0:
                state[x, pair, 27 * 8 :, :] = jnp.zeros((5 * 8, LANES), jnp.float32)

    stream_rows(before, x_low, x_high, y_low, y_high, sides, write)
    tangent_collide(state, post, (below, above, side_low, side_high), slope_one, slope_two, one, two, three)


def tangent_last(z_depth, probe_cells, probe_counts, before, x_low, x_high, y_low, y_high, out, rows_out, observed, sides):
    pairs = before.shape[1]
    rows_y = 8
    sums = {}

    def write(x, q, parts):
        vector = LATTICE[q]
        for pair in range(pairs):
            out[q, x, :, pair * LANES : (pair + 1) * LANES] = parts[pair]
            held = sums.setdefault((pair,), [None] * 4) if q else sums.__setitem__((pair,), [None] * 4) or sums[(pair,)]
            for m, factor in enumerate((1,) + vector):
                if factor == 0:
                    continue
                if held[m] is None:
                    held[m] = parts[pair] if factor == 1 else -parts[pair]
                else:
                    held[m] = held[m] + parts[pair] if factor == 1 else held[m] - parts[pair]
            if q == 26:
                for m in range(4):
                    observed[m, pair, pl.ds(pl.multiple_of(x * rows_y, rows_y), rows_y), :] = held[m]

    stream_rows(before, x_low, x_high, y_low, y_high, sides, write)
    peers, slots = probe_cells.shape
    left = lane_iota(1) < LANES // 2

    def probe(peer, carry):
        for slot in range(slots):
            cell = jnp.clip(probe_cells[peer, slot], 0, observed.shape[2] * z_depth - 1)
            place, z = cell // z_depth, cell % z_depth
            pair, odd = z // 2, z % 2
            live = slot < probe_counts[0, peer]
            rows = [observed[m, pair, pl.ds(place, 1), :] for m in range(4)]
            turned = [pltpu.roll(r, LANES // 2, 1) for r in rows]
            for m in (0, 2):
                low = jnp.where(odd == 1, turned[m], rows[m])
                high = jnp.where(odd == 1, rows[m + 1], turned[m + 1])
                value = jnp.where(left, low, high)
                rows_out[peer, slot : slot + 1, m * 64 : m * 64 + LANES] = jnp.where(live, value, 0.0)
        return carry

    lax.fori_loop(0, peers, probe, 0, unroll=2)


def shifts(axis, wrap):
    n = lax.axis_size(axis)
    up = [(i, (i + 1) % n) for i in range(n if wrap else n - 1)]
    return up, [(j, i) for i, j in up]


def spread(first, last, sides):
    x_low, x_high = first
    low_corner, high_corner, side_low, side_high = last
    up, down = sides
    pad = jnp.zeros((6, 1) + side_low.shape[2:], side_low.dtype)

    def full(side, low, high):
        return jnp.concatenate(
            [jnp.concatenate([pad, low], axis=0), side, jnp.concatenate([high, pad], axis=0)], axis=1
        )

    y_low = lax.ppermute(full(side_high, low_corner[0], high_corner[0]), "gy", up)
    y_high = lax.ppermute(full(side_low, low_corner[1], high_corner[1]), "gy", down)
    return x_low, x_high, y_low, y_high


def edge_rows(below, above, inflow, own_last):
    column, columns = lax.axis_index("gx"), lax.axis_size("gx")
    up, down = shifts("gx", False)
    x_low = jnp.where(column == 0, inflow, lax.ppermute(above, "gx", up))
    x_high = jnp.where(column == columns - 1, own_last, lax.ppermute(below, "gx", down))
    return x_low, x_high


def primal_halo(post, inflow):
    rows_x = post.shape[1]
    x_low, x_high = edge_rows(post[:9, :1], post[18:, rows_x - 1 :], inflow, post[:9, rows_x - 1 :])
    cut = post.reshape((3, 3, 3) + post.shape[1:])
    side = [cut[:, way].reshape((9,) + post.shape[1:]) for way in (0, 2)]
    return spread(
        (x_low, x_high), ((x_low[6:], x_low[:3]), (x_high[6:], x_high[:3]), side[0], side[1]), shifts("gy", True)
    )


def tangent_halo(last_row, below, above, side_low, side_high, inflow):
    x_low, x_high = edge_rows(below, above, inflow, last_row)
    return spread(
        (x_low, x_high),
        ((x_low[6:, -1:], x_low[:3, :1]), (x_high[6:, -1:], x_high[:3, :1]), side_low, side_high),
        shifts("gy", True),
    )


def shape(*dims):
    return jax.ShapeDtypeStruct(dims, jnp.float32)


def call(body, outs, scratch=(), specs=None, cost=None, **more):
    return pl.pallas_call(
        body,
        out_shape=outs,
        **({} if specs is None else {"in_specs": specs}),
        scratch_shapes=list(scratch),
        compiler_params=pltpu.CompilerParams(vmem_limit_bytes=VMEM_LIMIT),
        cost_estimate=cost,
        **more,
    )


def on_device(primal_pops, tangent_pops, inflow_pops, inflow_sens, w_in, b_in, w_mid, b_mid, w_out, b_out,
              probe_cells, probe_counts):
    rows_x, rows_y, z_depth = primal_pops.shape[1:]
    width = tangent_pops.shape[3]
    pairs = width // LANES
    hidden = w_in.shape[0]
    row_at = lax.axis_index("gy") * rows_y

    w_in = jnp.pad(w_in, ((0, 0), (0, QS - 27)))
    w_out = jnp.pad(w_out, ((0, QS - 27), (0, 0)))
    weights = (w_in, b_in[:, None], w_mid, b_mid[:, None], w_out, jnp.pad(b_out, (0, QS - 27))[:, None])
    tall = ((0, 0), (0, 0), (0, LANES - z_depth * rows_y))
    cells = jnp.pad(jnp.swapaxes(primal_pops, 2, 3).reshape(27, rows_x, z_depth * rows_y), tall)
    inflow = lax.dynamic_slice_in_dim(inflow_pops, row_at, rows_y, 1)
    inflow = jnp.pad(jnp.swapaxes(inflow, 1, 2).reshape(9, 1, z_depth * rows_y), tall)
    sens = lax.dynamic_slice_in_dim(inflow_sens, row_at, rows_y, 1)

    primal_outs = (shape(27, rows_x, LANES), shape(rows_x, hidden, LANES), shape(rows_x, hidden, LANES))
    primal_scratch = [pltpu.VMEM((QS * rows_x, LANES), jnp.float32)]
    tangent_outs = (
        shape(rows_x, pairs, QS * rows_y, LANES),
        shape(9, rows_y, width),
        shape(9, rows_y, width),
        shape(9, rows_x, width),
        shape(9, rows_x, width),
    )
    tangent_scratch = [
        pltpu.VMEM((rows_x, pairs, QS * rows_y, LANES), jnp.float32),
        pltpu.VMEM((hidden, 3 * QS), jnp.bfloat16),
        pltpu.VMEM((2 * hidden, 2 * hidden), jnp.bfloat16),
        pltpu.VMEM((2 * QS, 2 * hidden), jnp.bfloat16),
    ]
    sides = pltpu.VMEM((2, 9, pairs, rows_x + 8, LANES), jnp.float32)
    cost = pl.CostEstimate(flops=40 * 10**9, bytes_accessed=20 * 10**6, transcendentals=0)

    post, slope_one, slope_two = call(primal_first, primal_outs, primal_scratch)(cells, *weights)
    tangent = call(tangent_first, tangent_outs, tangent_scratch, cost=cost)(
        tangent_pops, slope_one, slope_two, w_in, w_mid, w_out
    )
    for step in range(1, STEPS):
        post, slope_one, slope_two = call(
            functools.partial(primal_next, z_depth), primal_outs, primal_scratch
        )(post, *primal_halo(post, inflow), *weights)
        state, *faces = tangent
        halo = tangent_halo(last_row(state, rows_x, rows_y), *faces, sens)
        tangent = call(tangent_next, tangent_outs, tangent_scratch + [sides], cost=cost)(
            state, *halo, slope_one, slope_two, w_in, w_mid, w_out
        )
    primal = call(functools.partial(primal_last, z_depth), shape(27, rows_x, LANES))(
        post, *primal_halo(post, inflow)
    )
    primal = jnp.swapaxes(primal[:, :, : z_depth * rows_y].reshape(27, rows_x, z_depth, rows_y), 2, 3)
    state, *faces = tangent
    halo = tangent_halo(last_row(state, rows_x, rows_y), *faces, sens)
    peers, slots = probe_cells.shape[1:]
    smem = pl.BlockSpec(memory_space=pltpu.SMEM)
    vmem = pl.BlockSpec(memory_space=pltpu.VMEM)
    tangent, jac = call(
        functools.partial(tangent_last, z_depth),
        (shape(27, rows_x, rows_y, width), shape(peers, slots, 4 * width // z_depth)),
        [pltpu.VMEM((4, pairs, rows_x * rows_y, LANES), jnp.float32), sides],
        specs=[smem, smem] + [vmem] * 5,
    )(probe_cells[0], probe_counts, state, *halo)
    jac = lax.all_to_all(jac[None], ("gx", "gy"), split_axis=1, concat_axis=1, tiled=True)
    return primal, tangent, jac


def last_row(state, rows_x, rows_y):
    row = state[rows_x - 1, :, : 9 * rows_y]
    return jnp.transpose(row.reshape(-1, 9, rows_y, LANES), (1, 2, 0, 3)).reshape(9, rows_y, -1)


def solution(mesh):
    both = P(("gx", "gy"))
    split_xy = P(None, "gx", "gy", None)
    return jax.shard_map(
        on_device,
        mesh=mesh,
        in_specs=(split_xy, split_xy) + (P(),) * 8 + (both, both),
        out_specs=(split_xy, split_xy, both),
        check_vma=False,
    )
```

profile of v0, /device:TPU:0, one launch (start us, length us, event | category | flops | bytes accessed | tf_op | source)
XLA Modules:
  0.0 214.4 jit_solution(13730214504154208747)
XLA Ops:
  2.1 1.3 pad.38.w_out
  3.4 1.4 copy.50.b_in
  4.8 1.4 copy.51.b_mid
  7.5 1.2 copy.48
  9.5 12.4 %shard_map.139 = (f32[27,16,128]{2,1,0:T(8,128)}, f32[16,128,128]{2,1,0:T(8,128)}, f32[16,128,128]{2,1,0:T(8,128)}) custom-call(f32[27,16,128]{2,1,0:T(8,128)} %pad.36.cells, f32[128,32]{1,0:T(8,128)} %pad.37.w_in, f32[128,1]{1,0:T(8,128)} %copy.50.b_in, f32[128,128]{1,0:T(8,128)} %w_mid.7, f32[128,1]{1,0:T(8,128)} %copy.51.b_mid, f32[32,128]{1,0:T(8,128)} %pad.38.w_out, ...), custom_call_target="tpu_custom_call" | custom-call | tf_op jit(solution)/shard_map/pallas_call | solution.py:391
  22.7 1.3 collective-permute-start.1
  24.0 41.7 %shard_map.142 = (f32[16,3,256,128]{3,2,1,0:T(8,128)}, f32[9,8,384]{2,1,0:T(8,128)}, f32[9,8,384]{2,1,0:T(8,128)}, f32[9,16,384]{2,1,0:T(8,128)}, f32[9,16,384]{2,1,0:T(8,128)}) custom-call(f32[27,16,8,384]{3,2,1,0:T(8,128)} %cells.1, f32[16,128,128]{2,1,0:T(8,128)} %get-tuple-element.23.slope_one, f32[16,128,128]{2,1,0:T(8,128)} %get-tuple-element.24.slope_two, ...), custom_call_target="tpu_custom_call" | custom-call | flops 40000000000 | bytes 20000000 | tf_op jit(solution)/shard_map/pallas_call | solution.py:392
  65.7 1.3 collective-permute-start.9
  67.0 3.7 %collective-permute-start.8 = (f32[9,8,384]{2,1,0:T(8,128)}, f32[9,8,384]{2,1,0:T(8,128)S(1)}, u32[]{:S(2)}, u32[]{:S(2)}) collective-permute-start(f32[9,8,384]{2,1,0:T(8,128)} %get-tuple-element.26), channel_id=1, source_target_pairs={{0,8},{8,16},{16,24},{1,9},{9,17},{17,25},{2,10},{10,18},{18,26},{... | collective-permute-start | bytes 331784 | tf_op jit(solution)/shard_map/ppermute | solution.py:316
  70.8 4.5 %collective-permute-start = (f32[9,1,128]{2,1,0:T(1,128)S(1)}, f32[9,1,128]{2,1,0:T(1,128)S(1)}, u32[]{:S(2)}, u32[]{:S(2)}) collective-permute-start(f32[9,1,128]{2,1,0:T(1,128)S(1)} %get-tuple-element.51), channel_id=1, source_target_pairs={{0,8},{8,16},{16,24},{1,9},{9,17},{17,25},{2,10},{10,18},{18,26},{... | collective-permute-start | bytes 13832 | tf_op jit(solution)/shard_map/ppermute | solution.py:316
  76.1 2.2 %collective-permute-start.2 = (f32[9,18,128]{2,1,0:T(8,128)S(1)}, f32[9,18,128]{2,1,0:T(8,128)S(1)}, u32[]{:S(2)}, u32[]{:S(2)}) collective-permute-start(f32[9,18,128]{2,1,0:T(8,128)S(1)} %select_maximum_fusion.12), channel_id=1, source_target_pairs={{0,1},{1,2},{2,3},{3,4},{4,5},{5,6},{6,7},{7,0},{8,9},{9,10},{10,1... | collective-permute-start | bytes 248840 | tf_op jit(solution)/shard_map/ppermute | solution.py:308
  78.4 3.1 %collective-permute-start.3 = (f32[9,18,128]{2,1,0:T(8,128)S(1)}, f32[9,18,128]{2,1,0:T(8,128)S(1)}, u32[]{:S(2)}, u32[]{:S(2)}) collective-permute-start(f32[9,18,128]{2,1,0:T(8,128)S(1)} %fusion.1), channel_id=1, source_target_pairs={{1,0},{2,1},{3,2},{4,3},{5,4},{6,5},{7,6},{0,7},{9,8},{10,9},{11,1... | collective-permute-start | bytes 248840 | tf_op jit(solution)/shard_map/ppermute | solution.py:309
  83.4 1.0 select_maximum_fusion.4
  84.4 2.1 collective-permute-start.11
  89.5 12.8 %shard_map.140 = (f32[27,16,128]{2,1,0:T(8,128)}, f32[16,128,128]{2,1,0:T(8,128)}, f32[16,128,128]{2,1,0:T(8,128)}) custom-call(f32[27,16,128]{2,1,0:T(8,128)} %get-tuple-element.21.before, f32[9,1,128]{2,1,0:T(1,128)} %copy-done.12, f32[9,1,128]{2,1,0:T(1,128)} %copy-done.15, f32[9,18,128]{2,1,0:T(8,128)} %copy-done.8, f32[9,18,128]{2,1,0:T(8,128)} %copy-done.9, ...), custom_call_target="tpu_custom_call" | custom-call | tf_op jit(solution)/shard_map/pallas_call | solution.py:396
  103.0 1.3 collective-permute-start.5
  106.1 43.7 %shard_map.143 = (f32[16,3,256,128]{3,2,1,0:T(8,128)}, f32[9,8,384]{2,1,0:T(8,128)}, f32[9,8,384]{2,1,0:T(8,128)}, f32[9,16,384]{2,1,0:T(8,128)}, f32[9,16,384]{2,1,0:T(8,128)}) custom-call(f32[16,3,256,128]{3,2,1,0:T(8,128)} %get-tuple-element.25.before, f32[9,8,384]{2,1,0:T(8,128)} %copy-done.7, f32[9,8,384]{2,1,0:T(8,128)} %copy-done.6, ...), custom_call_target="tpu_custom_call" | custom-call | flops 40000000000 | bytes 20000000 | tf_op jit(solution)/shard_map/pallas_call | solution.py:401
  149.8 1.3 collective-permute-start.13
  152.0 3.7 %collective-permute-start.4 = (f32[9,1,128]{2,1,0:T(1,128)S(1)}, f32[9,1,128]{2,1,0:T(1,128)S(1)}, u32[]{:S(2)}, u32[]{:S(2)}) collective-permute-start(f32[9,1,128]{2,1,0:T(1,128)S(1)} %get-tuple-element.48), channel_id=1, source_target_pairs={{0,8},{8,16},{16,24},{1,9},{9,17},{17,25},{2,10},{10,18},{18,26},{... | collective-permute-start | bytes 13832 | tf_op jit(solution)/shard_map/ppermute | solution.py:316
  155.6 3.6 %collective-permute-start.12 = (f32[9,8,384]{2,1,0:T(8,128)}, f32[9,8,384]{2,1,0:T(8,128)S(1)}, u32[]{:S(2)}, u32[]{:S(2)}) collective-permute-start(f32[9,8,384]{2,1,0:T(8,128)} %get-tuple-element.33), channel_id=1, source_target_pairs={{0,8},{8,16},{16,24},{1,9},{9,17},{17,25},{2,10},{10,18},{18,26},{... | collective-permute-start | bytes 331784 | tf_op jit(solution)/shard_map/ppermute | solution.py:316
  161.4 1.0 select_maximum_fusion
  162.4 4.7 %collective-permute-start.15 = (f32[9,18,384]{2,1,0:T(8,128)S(1)}, f32[9,18,384]{2,1,0:T(8,128)S(1)}, u32[]{:S(2)}, u32[]{:S(2)}) collective-permute-start(f32[9,18,384]{2,1,0:T(8,128)S(1)} %select_maximum_fusion), channel_id=1, source_target_pairs={{1,0},{2,1},{3,2},{4,3},{5,4},{6,5},{7,6},{0,7},{9,8},{10,9},{11,1... | collective-permute-start | bytes 746504 | tf_op jit(solution)/shard_map/ppermute | solution.py:309
  167.1 1.0 select_maximum_fusion.2
  168.2 6.7 %collective-permute-done.15.y_high = f32[9,18,384]{2,1,0:T(8,128)S(1)} collective-permute-done((f32[9,18,384]{2,1,0:T(8,128)S(1)}, f32[9,18,384]{2,1,0:T(8,128)S(1)}, u32[]{:S(2)}, u32[]{:S(2)}) %collective-permute-start.15) | collective-permute-done | bytes 248864 | tf_op jit(solution)/shard_map/ppermute | solution.py:309
  174.9 6.5 %collective-permute-done.14.y_low = f32[9,18,384]{2,1,0:T(8,128)S(1)} collective-permute-done((f32[9,18,384]{2,1,0:T(8,128)S(1)}, f32[9,18,384]{2,1,0:T(8,128)S(1)}, u32[]{:S(2)}, u32[]{:S(2)}) %collective-permute-start.14) | collective-permute-done | bytes 248864 | tf_op jit(solution)/shard_map/ppermute | solution.py:308
  182.1 10.3 %shard_map.144 = (f32[27,16,8,384]{3,2,1,0:T(8,128)}, f32[32,4,256]{2,1,0:T(4,128)}) custom-call(s32[32,4]{1,0:T(8,128)} %copy.64.probe_cells, s32[1,32]{1,0:T(1,128)} %probe_counts.1, f32[16,3,256,128]{3,2,1,0:T(8,128)} %get-tuple-element.32.before, f32[9,8,384]{2,1,0:T(8,128)} %copy-done.3, f32[9,8,384]{2,1,0:T(8,128)} %copy-done.2, ...), custom_call_target="tpu_custom_call" | custom-call | tf_op jit(solution)/shard_map/pallas_call | solution.py:413
  192.4 4.5 %all-to-all-start = ((f32[1,32,4,256]{3,2,0,1:T(4,128)}), f32[1,32,4,256]{3,2,0,1:T(4,128)S(1)}, u32[]{:S(2)}, u32[]{:S(2)}) async-start(f32[1,32,4,256]{3,2,0,1:T(4,128)} %bitcast.56), calls=%async_computation | async-start | bytes 262144 | tf_op jit(solution)/shard_map/all_to_all | solution.py:419
  197.0 4.6 %collective-permute-start.7 = (f32[9,18,128]{2,1,0:T(8,128)S(1)}, f32[9,18,128]{2,1,0:T(8,128)S(1)}, u32[]{:S(2)}, u32[]{:S(2)}) collective-permute-start(f32[9,18,128]{2,1,0:T(8,128)S(1)} %fusion), channel_id=1, source_target_pairs={{1,0},{2,1},{3,2},{4,3},{5,4},{6,5},{7,6},{0,7},{9,8},{10,9},{11,1... | collective-permute-start | bytes 248840 | tf_op jit(solution)/shard_map/ppermute | solution.py:309
  201.7 2.5 %collective-permute-done.7.y_high = f32[9,18,128]{2,1,0:T(8,128)S(1)} collective-permute-done((f32[9,18,128]{2,1,0:T(8,128)S(1)}, f32[9,18,128]{2,1,0:T(8,128)S(1)}, u32[]{:S(2)}, u32[]{:S(2)}) %collective-permute-start.7) | collective-permute-done | bytes 82976 | tf_op jit(solution)/shard_map/ppermute | solution.py:309
  204.2 5.0 %collective-permute-done.6.y_low = f32[9,18,128]{2,1,0:T(8,128)S(1)} collective-permute-done((f32[9,18,128]{2,1,0:T(8,128)S(1)}, f32[9,18,128]{2,1,0:T(8,128)S(1)}, u32[]{:S(2)}, u32[]{:S(2)}) %collective-permute-start.6) | collective-permute-done | bytes 82976 | tf_op jit(solution)/shard_map/ppermute | solution.py:308
  209.8 2.0 shard_map.141
  211.8 1.9 copy.61
  (90 shorter events, 17.7 us)
Async XLA Ops:
  0.6 74.7 %copy-start = (f32[9,64,6]{1,2,0:T(8,128)S(1)}, f32[9,64,6]{1,2,0:T(8,128)}, u32[]{:S(2)}) copy-start(f32[9,64,6]{1,2,0:T(8,128)} %param.14) | copy-start | bytes 41476
  22.7 48.0 %collective-permute-start.1 = (f32[9,1,128]{2,1,0:T(1,128)S(1)}, f32[9,1,128]{2,1,0:T(1,128)S(1)}, u32[]{:S(2)}, u32[]{:S(2)}) collective-permute-start(f32[9,1,128]{2,1,0:T(1,128)S(1)} %slice.87), channel_id=1, source_target_pairs={{8,0},{16,8},{24,16},{9,1},{17,9},{25,17},{10,2},{18,10},{26,18},{... | collective-permute-start | bytes 13832 | tf_op jit(solution)/shard_map/ppermute | solution.py:317
  24.0 46.7 %copy-start.1 = (f32[27,16,128]{2,1,0:T(8,128)S(1)}, f32[27,16,128]{2,1,0:T(8,128)}, u32[]{:S(2)}) copy-start(f32[27,16,128]{2,1,0:T(8,128)} %get-tuple-element.21.before) | copy-start | bytes 663556
  24.0 46.7 %copy-start.16 = (pred[9]{0:T(512)(128)(4,1)S(1)}, pred[9]{0:T(512)(128)(4,1)}, u32[]{:S(2)}) copy-start(pred[9]{0:T(512)(128)(4,1)} %constant.22.clone.1) | copy-start | bytes 31
  24.0 63.5 %copy-start.17 = (s32[1,32,4]{1,2,0:T(4,128)S(1)}, s32[1,32,4]{1,2,0:T(4,128)}, u32[]{:S(2)}) copy-start(s32[1,32,4]{1,2,0:T(4,128)} %param.22) | copy-start | bytes 1540
  65.7 15.8 %collective-permute-start.9 = (f32[9,8,384]{2,1,0:T(8,128)}, f32[9,8,384]{2,1,0:T(8,128)S(1)}, u32[]{:S(2)}, u32[]{:S(2)}) collective-permute-start(f32[9,8,384]{2,1,0:T(8,128)} %get-tuple-element.27), channel_id=1, source_target_pairs={{8,0},{16,8},{24,16},{9,1},{17,9},{25,17},{10,2},{18,10},{26,18},{... | collective-permute-start | bytes 331784 | tf_op jit(solution)/shard_map/ppermute | solution.py:317
  67.0 15.5 %collective-permute-start.8 = (f32[9,8,384]{2,1,0:T(8,128)}, f32[9,8,384]{2,1,0:T(8,128)S(1)}, u32[]{:S(2)}, u32[]{:S(2)}) collective-permute-start(f32[9,8,384]{2,1,0:T(8,128)} %get-tuple-element.26), channel_id=1, source_target_pairs={{0,8},{8,16},{16,24},{1,9},{9,17},{17,25},{2,10},{10,18},{18,26},{... | collective-permute-start | bytes 331784 | tf_op jit(solution)/shard_map/ppermute | solution.py:316
  70.8 17.4 %copy-start.15 = (f32[9,1,128]{2,1,0:T(1,128)}, f32[9,1,128]{2,1,0:T(1,128)S(1)}, u32[]{:S(2)}) copy-start(f32[9,1,128]{2,1,0:T(1,128)S(1)} %get-tuple-element.45.x_high) | copy-start | bytes 13828
  70.8 5.3 %collective-permute-start = (f32[9,1,128]{2,1,0:T(1,128)S(1)}, f32[9,1,128]{2,1,0:T(1,128)S(1)}, u32[]{:S(2)}, u32[]{:S(2)}) collective-permute-start(f32[9,1,128]{2,1,0:T(1,128)S(1)} %get-tuple-element.51), channel_id=1, source_target_pairs={{0,8},{8,16},{16,24},{1,9},{9,17},{17,25},{2,10},{10,18},{18,26},{... | collective-permute-start | bytes 13832 | tf_op jit(solution)/shard_map/ppermute | solution.py:316
  76.1 12.1 %copy-start.12 = (f32[9,1,128]{2,1,0:T(1,128)}, f32[9,1,128]{2,1,0:T(1,128)S(1)}, u32[]{:S(2)}) copy-start(f32[9,1,128]{2,1,0:T(1,128)S(1)} %broadcast_select_fusion.3.x_low) | copy-start | bytes 13828
  76.1 12.1 %collective-permute-start.2 = (f32[9,18,128]{2,1,0:T(8,128)S(1)}, f32[9,18,128]{2,1,0:T(8,128)S(1)}, u32[]{:S(2)}, u32[]{:S(2)}) collective-permute-start(f32[9,18,128]{2,1,0:T(8,128)S(1)} %select_maximum_fusion.12), channel_id=1, source_target_pairs={{0,1},{1,2},{2,3},{3,4},{4,5},{5,6},{6,7},{7,0},{8,9},{9,10},{10,1... | collective-permute-start | bytes 248840 | tf_op jit(solution)/shard_map/ppermute | solution.py:308
  78.4 9.9 %collective-permute-start.3 = (f32[9,18,128]{2,1,0:T(8,128)S(1)}, f32[9,18,128]{2,1,0:T(8,128)S(1)}, u32[]{:S(2)}, u32[]{:S(2)}) collective-permute-start(f32[9,18,128]{2,1,0:T(8,128)S(1)} %fusion.1), channel_id=1, source_target_pairs={{1,0},{2,1},{3,2},{4,3},{5,4},{6,5},{7,6},{0,7},{9,8},{10,9},{11,1... | collective-permute-start | bytes 248840 | tf_op jit(solution)/shard_map/ppermute | solution.py:309
  82.4 22.9 %copy-start.6 = (f32[9,8,384]{2,1,0:T(8,128)}, f32[9,8,384]{2,1,0:T(8,128)S(1)}, u32[]{:S(2)}) copy-start(f32[9,8,384]{2,1,0:T(8,128)S(1)} %bitcast_select_fusion.1.x_high) | copy-start | bytes 331780
  83.4 22.0 %copy-start.7 = (f32[9,8,384]{2,1,0:T(8,128)}, f32[9,8,384]{2,1,0:T(8,128)S(1)}, u32[]{:S(2)}) copy-start(f32[9,8,384]{2,1,0:T(8,128)S(1)} %dynamic-slice_select_fusion.1.x_low) | copy-start | bytes 331780
  84.4 20.9 %collective-permute-start.11 = (f32[9,18,384]{2,1,0:T(8,128)S(1)}, f32[9,18,384]{2,1,0:T(8,128)S(1)}, u32[]{:S(2)}, u32[]{:S(2)}) collective-permute-start(f32[9,18,384]{2,1,0:T(8,128)S(1)} %select_maximum_fusion.4), channel_id=1, source_target_pairs={{1,0},{2,1},{3,2},{4,3},{5,4},{6,5},{7,6},{0,7},{9,8},{10,9},{11,1... | collective-permute-start | bytes 746504 | tf_op jit(solution)/shard_map/ppermute | solution.py:309
  87.4 17.8 %collective-permute-start.10 = (f32[9,18,384]{2,1,0:T(8,128)S(1)}, f32[9,18,384]{2,1,0:T(8,128)S(1)}, u32[]{:S(2)}, u32[]{:S(2)}) collective-permute-start(f32[9,18,384]{2,1,0:T(8,128)S(1)} %select_maximum_fusion.6), channel_id=1, source_target_pairs={{0,1},{1,2},{2,3},{3,4},{4,5},{5,6},{6,7},{7,0},{8,9},{9,10},{10,1... | collective-permute-start | bytes 746504 | tf_op jit(solution)/shard_map/ppermute | solution.py:308
  103.0 48.0 %collective-permute-start.5 = (f32[9,1,128]{2,1,0:T(1,128)S(1)}, f32[9,1,128]{2,1,0:T(1,128)S(1)}, u32[]{:S(2)}, u32[]{:S(2)}) collective-permute-start(f32[9,1,128]{2,1,0:T(1,128)S(1)} %slice.95), channel_id=1, source_target_pairs={{8,0},{16,8},{24,16},{9,1},{17,9},{25,17},{10,2},{18,10},{26,18},{... | collective-permute-start | bytes 13832 | tf_op jit(solution)/shard_map/ppermute | solution.py:317
  105.3 0.8 copy-start.19
  149.8 9.5 %collective-permute-start.13 = (f32[9,8,384]{2,1,0:T(8,128)}, f32[9,8,384]{2,1,0:T(8,128)S(1)}, u32[]{:S(2)}, u32[]{:S(2)}) collective-permute-start(f32[9,8,384]{2,1,0:T(8,128)} %get-tuple-element.34), channel_id=1, source_target_pairs={{8,0},{16,8},{24,16},{9,1},{17,9},{25,17},{10,2},{18,10},{26,18},{... | collective-permute-start | bytes 331784 | tf_op jit(solution)/shard_map/ppermute | solution.py:317
  152.0 57.2 %copy-start.14 = (f32[9,1,128]{2,1,0:T(1,128)}, f32[9,1,128]{2,1,0:T(1,128)S(1)}, u32[]{:S(2)}) copy-start(f32[9,1,128]{2,1,0:T(1,128)S(1)} %get-tuple-element.43.x_high) | copy-start | bytes 13828
  152.0 16.2 %collective-permute-start.4 = (f32[9,1,128]{2,1,0:T(1,128)S(1)}, f32[9,1,128]{2,1,0:T(1,128)S(1)}, u32[]{:S(2)}, u32[]{:S(2)}) collective-permute-start(f32[9,1,128]{2,1,0:T(1,128)S(1)} %get-tuple-element.48), channel_id=1, source_target_pairs={{0,8},{8,16},{16,24},{1,9},{9,17},{17,25},{2,10},{10,18},{18,26},{... | collective-permute-start | bytes 13832 | tf_op jit(solution)/shard_map/ppermute | solution.py:316
  155.6 4.8 %collective-permute-start.12 = (f32[9,8,384]{2,1,0:T(8,128)}, f32[9,8,384]{2,1,0:T(8,128)S(1)}, u32[]{:S(2)}, u32[]{:S(2)}) collective-permute-start(f32[9,8,384]{2,1,0:T(8,128)} %get-tuple-element.33), channel_id=1, source_target_pairs={{0,8},{8,16},{16,24},{1,9},{9,17},{17,25},{2,10},{10,18},{18,26},{... | collective-permute-start | bytes 331784 | tf_op jit(solution)/shard_map/ppermute | solution.py:316
  160.2 21.2 %copy-start.2 = (f32[9,8,384]{2,1,0:T(8,128)}, f32[9,8,384]{2,1,0:T(8,128)S(1)}, u32[]{:S(2)}) copy-start(f32[9,8,384]{2,1,0:T(8,128)S(1)} %bitcast_select_fusion.x_high) | copy-start | bytes 331780
  161.4 20.0 %copy-start.3 = (f32[9,8,384]{2,1,0:T(8,128)}, f32[9,8,384]{2,1,0:T(8,128)S(1)}, u32[]{:S(2)}) copy-start(f32[9,8,384]{2,1,0:T(8,128)S(1)} %dynamic-slice_select_fusion.x_low) | copy-start | bytes 331780
  162.4 12.5 %collective-permute-start.15 = (f32[9,18,384]{2,1,0:T(8,128)S(1)}, f32[9,18,384]{2,1,0:T(8,128)S(1)}, u32[]{:S(2)}, u32[]{:S(2)}) collective-permute-start(f32[9,18,384]{2,1,0:T(8,128)S(1)} %select_maximum_fusion), channel_id=1, source_target_pairs={{1,0},{2,1},{3,2},{4,3},{5,4},{6,5},{7,6},{0,7},{9,8},{10,9},{11,1... | collective-permute-start | bytes 746504 | tf_op jit(solution)/shard_map/ppermute | solution.py:309
  168.1 13.3 %collective-permute-start.14 = (f32[9,18,384]{2,1,0:T(8,128)S(1)}, f32[9,18,384]{2,1,0:T(8,128)S(1)}, u32[]{:S(2)}, u32[]{:S(2)}) collective-permute-start(f32[9,18,384]{2,1,0:T(8,128)S(1)} %select_maximum_fusion.2), channel_id=1, source_target_pairs={{0,1},{1,2},{2,3},{3,4},{4,5},{5,6},{6,7},{7,0},{8,9},{9,10},{10,1... | collective-permute-start | bytes 746504 | tf_op jit(solution)/shard_map/ppermute | solution.py:308
  168.2 40.9 %copy-start.13 = (f32[9,1,128]{2,1,0:T(1,128)}, f32[9,1,128]{2,1,0:T(1,128)S(1)}, u32[]{:S(2)}) copy-start(f32[9,1,128]{2,1,0:T(1,128)S(1)} %broadcast_select_fusion.2.x_low) | copy-start | bytes 13828
  174.9 6.5 %copy-start.4 = (f32[9,18,384]{2,1,0:T(8,128)}, f32[9,18,384]{2,1,0:T(8,128)S(1)}, u32[]{:S(2)}) copy-start(f32[9,18,384]{2,1,0:T(8,128)S(1)} %collective-permute-done.15.y_high) | copy-start | bytes 746500
  192.4 21.3 %all-to-all-start = ((f32[1,32,4,256]{3,2,0,1:T(4,128)}), f32[1,32,4,256]{3,2,0,1:T(4,128)S(1)}, u32[]{:S(2)}, u32[]{:S(2)}) async-start(f32[1,32,4,256]{3,2,0,1:T(4,128)} %bitcast.56), calls=%async_computation | async-start | bytes 262144 | tf_op jit(solution)/shard_map/all_to_all | solution.py:419
  197.0 7.2 %collective-permute-start.7 = (f32[9,18,128]{2,1,0:T(8,128)S(1)}, f32[9,18,128]{2,1,0:T(8,128)S(1)}, u32[]{:S(2)}, u32[]{:S(2)}) collective-permute-start(f32[9,18,128]{2,1,0:T(8,128)S(1)} %fusion), channel_id=1, source_target_pairs={{1,0},{2,1},{3,2},{4,3},{5,4},{6,5},{7,6},{0,7},{9,8},{10,9},{11,1... | collective-permute-start | bytes 248840 | tf_op jit(solution)/shard_map/ppermute | solution.py:309
  201.6 7.6 %collective-permute-start.6 = (f32[9,18,128]{2,1,0:T(8,128)S(1)}, f32[9,18,128]{2,1,0:T(8,128)S(1)}, u32[]{:S(2)}, u32[]{:S(2)}) collective-permute-start(f32[9,18,128]{2,1,0:T(8,128)S(1)} %select_maximum_fusion.9), channel_id=1, source_target_pairs={{0,1},{1,2},{2,3},{3,4},{4,5},{5,6},{6,7},{7,0},{8,9},{9,10},{10,1... | collective-permute-start | bytes 248840 | tf_op jit(solution)/shard_map/ppermute | solution.py:308
  204.2 5.0 %copy-start.10 = (f32[9,18,128]{2,1,0:T(8,128)}, f32[9,18,128]{2,1,0:T(8,128)S(1)}, u32[]{:S(2)}) copy-start(f32[9,18,128]{2,1,0:T(8,128)S(1)} %collective-permute-done.7.y_high) | copy-start | bytes 248836
  (5 other events, 3.4 us)
where the time goes:
time: 215 us; the launch traced here: 214 us
  Pallas kernels  123 us (57%)
  starting transfers between devices  42 us (20%)
  waiting for transfers between devices  21.5 us (10%)
  local copies, waits for them, and re-layouts  18.2 us (8%)
  other arithmetic  8.69 us (4%)
    pallas_call x1, Pallas kernels, on_device(): call(tangent_next, tangent_outs, tangent_scratch + [sides], cost=cost)  43.7 us
    pallas_call x1, Pallas kernels, on_device(): call(tangent_first, tangent_outs, tangent_scratch, cost=cost)  41.7 us
    ppermute x4, starting transfers between devices, edge_rows(): x_low = jnp.where(column == 0, inflow, lax.ppermute(above, 'gx', up))  15.5 us
    ppermute x4, starting transfers between devices, spread(): lax.ppermute(full(side_low, low_corner[1], high_corner[1]), 'gy', down)  14.5 us
    pallas_call x1, Pallas kernels, on_device(): call(functools.partial(primal_next, z_depth), primal_outs, primal_scratch)  12.8 us
    pallas_call x1, Pallas kernels, on_device(): call(primal_first, primal_outs, primal_scratch)(cells, *weights)  12.4 us
    ppermute x4, waiting for transfers between devices, spread(): lax.ppermute(full(side_high, low_corner[0], high_corner[0]), 'gy', up)  11.5 us
    pallas_call x1, Pallas kernels, on_device(): call(functools.partial(tangent_last, z_depth), (shape(27, rows_x, rows_y,...  10.3 us
  transfers between devices with their start and end apart: 17, of which 6 were waited for; matrix products, arithmetic and copies ran while one was open for 6% of the time, Pallas kernels for 47%

commit v1 on v0

v1 whole, which is shorter than its diff:
```python
import functools

import jax
import jax.numpy as jnp
from jax import lax
from jax.experimental import pallas as pl
from jax.experimental.pallas import tpu as pltpu
from jax.sharding import PartitionSpec as P

STEPS = 2
QS = 32
LANES = 128
GROUP = 6
VMEM_LIMIT = 60 * 1024 * 1024
LATTICE = [(q // 9 - 1, q // 3 % 3 - 1, q % 3 - 1) for q in range(27)]


def split(value):
    high = value.astype(jnp.bfloat16)
    low = (value - high.astype(jnp.float32)).astype(jnp.bfloat16)
    return high, low


def dot(a, b):
    return jnp.dot(a, b, preferred_element_type=jnp.float32)


def lane_iota(rows):
    return lax.broadcasted_iota(jnp.int32, (rows, LANES), 1)


def make_weights(w_in, w_mid, w_out, one, two, three):
    high, low = split(w_in[...])
    one[...] = jnp.concatenate([high, high, low], axis=1)
    high, low = split(w_mid[...])
    two[...] = jnp.concatenate(
        [jnp.concatenate([high, high], axis=1), jnp.concatenate([low, jnp.zeros_like(low)], axis=1)], axis=0
    )
    high, low = split(w_out[...])
    three[...] = jnp.concatenate(
        [jnp.concatenate([high, high], axis=1), jnp.concatenate([low, jnp.zeros_like(low)], axis=1)], axis=0
    )


def primal_stream(post_ref, x_rows, y_sides, write, z_depth):
    rows_x, rows_y = post_ref.shape[1], 8
    lane = lane_iota(rows_x)
    at_y = lane % rows_y
    last_z = (z_depth - 1) * rows_y
    for q, (ex, ey, ez) in enumerate(LATTICE):
        own = post_ref[q]
        if ex == 1:
            own = jnp.concatenate([x_rows[0, q - 18 : q - 17, :], own[: rows_x - 1]], axis=0)
        elif ex == -1:
            own = jnp.concatenate([own[1:], x_rows[1, q : q + 1, :]], axis=0)
        if ey != 0:
            j = (ex + 1) * 3 + ez + 1
            side = y_sides[0 if ey == 1 else 1, j, 1 - ex : 1 - ex + rows_x, :]
            if ey == 1:
                own = jnp.where(at_y == 0, pltpu.roll(side, LANES - rows_y + 1, 1), pltpu.roll(own, 1, 1))
            else:
                own = jnp.where(at_y == rows_y - 1, pltpu.roll(side, rows_y - 1, 1), pltpu.roll(own, LANES - 1, 1))
        if ez == 1:
            own = jnp.where(lane < rows_y, post_ref[26 - q], pltpu.roll(own, rows_y, 1))
        elif ez == -1:
            own = jnp.where(lane >= last_z, post_ref[26 - q], pltpu.roll(own, LANES - rows_y, 1))
        write(q, own)


def stream_rows(before, x_rows, sides, write):
    rows_x, pairs = before.shape[0], before.shape[1]
    rows_y = 8
    lane = lane_iota(rows_y)
    left = lane < LANES // 2
    at_y = lax.broadcasted_iota(jnp.int32, (rows_y, LANES), 0)
    def one_row(x, edge):
        for q, (ex, ey, ez) in enumerate(LATTICE):
            parts = []
            for pair in range(pairs):
                if edge == -1 and ex == 1:
                    value = x_rows[0, q - 18, pair]
                elif edge == 1 and ex == -1:
                    value = x_rows[1, q, pair]
                else:
                    value = before[x - ex, pair, q * rows_y : (q + 1) * rows_y, :]
                if ey != 0:
                    j = (ex + 1) * 3 + ez + 1
                    side = sides[0 if ey == 1 else 1, j, pair, pl.ds(x - ex + 1, 1), :]
                    if ey == 1:
                        value = jnp.where(at_y == 0, side, pltpu.roll(value, 1, 0))
                    else:
                        value = jnp.where(at_y == rows_y - 1, side, pltpu.roll(value, rows_y - 1, 0))
                parts.append(value)
            if ez != 0:
                turned = [pltpu.roll(part, LANES // 2, 1) for part in parts]
                mirror = 26 - q
                if ez == 1:
                    wall = before[x, 0, mirror * rows_y : (mirror + 1) * rows_y, :]
                    parts = [jnp.where(left, turned[p - 1] if p else wall, turned[p]) for p in range(pairs)]
                else:
                    wall = before[x, pairs - 1, mirror * rows_y : (mirror + 1) * rows_y, :]
                    parts = [jnp.where(left, turned[p], turned[p + 1] if p + 1 < pairs else wall) for p in range(pairs)]
            write(x, q, parts)

    one_row(0, -1)

    def inner(x, carry):
        one_row(x, 0)
        return carry

    lax.fori_loop(1, rows_x - 1, inner, 0)
    one_row(rows_x - 1, 1)


def primal_collide(state_ref, biases, post_ref, slope_one_ref, slope_two_ref, one, two, three):
    b_in, b_mid, b_out = biases
    rows_x = post_ref.shape[1]
    hidden = two.shape[0] // 2

    def row(x, carry):
        cell = state_ref[pl.ds(x, QS, stride=rows_x), :]
        high, low = split(cell)
        act_one = jnp.tanh(dot(one[...], jnp.concatenate([high, low, high], axis=0)) + b_in[...])
        high, low = split(act_one)
        second = dot(two[...], jnp.concatenate([high, low], axis=0))
        act_two = jnp.tanh(second[:hidden] + second[hidden:] + b_mid[...])
        high, low = split(act_two)
        moved = dot(three[...], jnp.concatenate([high, low], axis=0))
        slope_one_ref[x] = 1.0 - act_one * act_one
        slope_two_ref[x] = 1.0 - act_two * act_two
        state_ref[pl.ds(x, QS, stride=rows_x), :] = cell + moved[:QS] + moved[QS:] + b_out[...]
        return carry

    lax.fori_loop(0, rows_x, row, 0, unroll=4)
    for q in range(27):
        post_ref[q] = state_ref[q * rows_x : (q + 1) * rows_x, :]


def collide_columns(x, columns, state, post, slope_one, slope_two, one, two, three):
    rows_y = 8
    hidden = two.shape[0] // 2
    half = lane_iota(hidden) < LANES // 2
    s_one, s_two = slope_one[x], slope_two[x]

    def scale(slopes, y, pair):
        left = slopes[:, 2 * pair * rows_y + y : 2 * pair * rows_y + y + 1]
        right = slopes[:, (2 * pair + 1) * rows_y + y : (2 * pair + 1) * rows_y + y + 1]
        return jnp.where(half, left, right)

    for start in range(0, len(columns), GROUP):
        here = columns[start : start + GROUP]
        cell = jnp.concatenate([state[x, pair, pl.ds(y, QS, stride=rows_y), :] for y, pair in here], axis=1)
        high, low = split(cell)
        lifted = dot(one[...], jnp.concatenate([high, low, high], axis=0))
        high, low = split(lifted * jnp.concatenate([scale(s_one, y, pair) for y, pair in here], axis=1))
        mixed = dot(two[...], jnp.concatenate([high, low], axis=0))
        mixed = mixed[:hidden] + mixed[hidden:]
        high, low = split(mixed * jnp.concatenate([scale(s_two, y, pair) for y, pair in here], axis=1))
        moved = dot(three[...], jnp.concatenate([high, low], axis=0))
        result = cell + moved[:QS] + moved[QS:]
        for i, (y, pair) in enumerate(here):
            post[x, pair, pl.ds(y, QS, stride=rows_y), :] = result[:, i * LANES : (i + 1) * LANES]


def exchange_and_collide(cell_state, state, weights, inflow, outs, scratch):
    w_in, b_in, w_mid, b_mid, w_out, b_out = weights
    cell_inflow, sens_inflow = inflow
    cell_post, cell_rows, cell_sides, post, x_rows, sides = outs
    (slope_one, slope_two, one, two, three, cell_edge, cell_face, edge, face,
     cell_edge_in, cell_face_in, cell_corner_in, edge_in, face_in, corner_in, send_sem, recv_sem) = scratch
    rows_x, pairs, rows_y = state.shape[0], state.shape[1], 8
    column, columns_x = lax.axis_index("gx"), lax.axis_size("gx")
    line, lines = lax.axis_index("gy"), lax.axis_size("gy")

    def at(dx, dy):
        return (lax.rem(column + dx + columns_x, columns_x), lax.rem(line + dy + lines, lines))

    barrier = pltpu.get_barrier_semaphore()
    for dx in (-1, 0, 1):
        for dy in (-1, 0, 1):
            if dx or dy:
                pl.semaphore_signal(barrier, inc=1, device_id=at(dx, dy), device_id_type=pl.DeviceIdType.MESH)

    copies = []

    def send(source, target, dx, dy):
        i = len(copies)
        copy = pltpu.make_async_remote_copy(
            src_ref=source, dst_ref=target, send_sem=send_sem.at[i], recv_sem=recv_sem.at[i],
            device_id=at(dx, dy), device_id_type=pl.DeviceIdType.MESH,
        )
        copy.start()
        copies.append(copy)

    make_weights(w_in, w_mid, w_out, one, two, three)
    primal_collide(cell_state, (b_in, b_mid, b_out), cell_post, slope_one, slope_two, one, two, three)
    cell_edge[0] = cell_state[pl.ds(0, 16, stride=rows_x), :]
    cell_edge[1, :9] = cell_state[pl.ds(18 * rows_x + rows_x - 1, 9, stride=rows_x), :]
    cell_edge[1, 9:] = jnp.zeros((7, LANES), jnp.float32)
    for ex in range(3):
        for ez in range(3):
            cell_face[1, ex * 3 + ez] = cell_post[ex * 9 + 6 + ez]
            cell_face[0, ex * 3 + ez] = cell_post[ex * 9 + ez]

    inner = [(y, pair) for y in range(1, rows_y - 1) for pair in range(pairs)]
    outer = [(y, pair) for y in (0, rows_y - 1) for pair in range(pairs)]

    def outer_row(x, carry):
        collide_columns(x, outer, state, post, slope_one, slope_two, one, two, three)
        return carry

    def inner_row(x, carry):
        collide_columns(x, inner, state, post, slope_one, slope_two, one, two, three)
        return carry

    def end_row(i, carry):
        return inner_row(i * (rows_x - 1), carry)

    lax.fori_loop(0, rows_x, outer_row, 0, unroll=4)
    lax.fori_loop(0, 2, end_row, 0)
    stride = pairs * QS * rows_y
    flat = post.reshape(rows_x * stride, LANES)
    for pair in range(pairs):
        for ex in range(3):
            for ez in range(3):
                q = ex * 9 + 6 + ez
                face[1, ex * 3 + ez, pair] = flat[pl.ds((pair * QS + q + 1) * rows_y - 1, rows_x, stride=stride), :]
                q = ex * 9 + ez
                face[0, ex * 3 + ez, pair] = flat[pl.ds((pair * QS + q) * rows_y, rows_x, stride=stride), :]
        for j in range(9):
            edge[0, j, pair] = post[0, pair, j * rows_y : (j + 1) * rows_y, :]
            edge[1, j, pair] = post[rows_x - 1, pair, (18 + j) * rows_y : (19 + j) * rows_y, :]

    pl.semaphore_wait(barrier, 8)
    send(face.at[1], face_in.at[0], 0, 1)
    send(face.at[0], face_in.at[1], 0, -1)
    send(edge.at[1], edge_in.at[0], 1, 0)
    send(edge.at[0], edge_in.at[1], -1, 0)
    send(edge.at[1, 6:9], corner_in.at[0], 1, 1)
    send(edge.at[0, 6:9], corner_in.at[1], -1, 1)
    send(edge.at[1, 0:3], corner_in.at[2], 1, -1)
    send(edge.at[0, 0:3], corner_in.at[3], -1, -1)
    send(cell_face.at[1], cell_face_in.at[0], 0, 1)
    send(cell_face.at[0], cell_face_in.at[1], 0, -1)
    send(cell_edge.at[1], cell_edge_in.at[0], 1, 0)
    send(cell_edge.at[0], cell_edge_in.at[1], -1, 0)
    send(cell_edge.at[1], cell_corner_in.at[0], 1, 1)
    send(cell_edge.at[0], cell_corner_in.at[1], -1, 1)
    send(cell_edge.at[1], cell_corner_in.at[2], 1, -1)
    send(cell_edge.at[0], cell_corner_in.at[3], -1, -1)

    lax.fori_loop(1, rows_x - 1, inner_row, 0)
    for copy in copies:
        copy.wait()

    first, last = column == 0, column == columns_x - 1
    end = rows_x + 1
    cell_rows[0] = jnp.where(first, cell_inflow[1], cell_edge_in[0])
    cell_rows[1] = jnp.where(last, cell_state[pl.ds(rows_x - 1, 16, stride=rows_x), :], cell_edge_in[1])
    for j in range(9):
        for way in range(2):
            cell_sides[way, j, 1:end] = cell_face_in[way, j]
        for pair in range(pairs):
            own = post[rows_x - 1, pair, j * rows_y : (j + 1) * rows_y, :]
            x_rows[0, j, pair] = jnp.where(first, sens_inflow[1, j, pair], edge_in[0, j, pair])
            x_rows[1, j, pair] = jnp.where(last, own, edge_in[1, j, pair])
            for way in range(2):
                sides[way, j, pair, 1:end] = face_in[way, j, pair]
    for way, take in ((0, 6), (1, 0)):
        y = rows_y - 1 if way == 0 else 0
        for i in range(3):
            k = take + i
            cell_sides[way, 6 + i, 0:1] = jnp.where(
                first, cell_inflow[2 * way, k : k + 1, :], cell_corner_in[2 * way, k : k + 1, :])
            cell_sides[way, i, end : end + 1] = jnp.where(
                last, cell_face_in[way, i, rows_x - 1 :, :], cell_corner_in[2 * way + 1, k : k + 1, :])
            for pair in range(pairs):
                sides[way, 6 + i, pair, 0:1] = jnp.where(
                    first, sens_inflow[2 * way, k, pair, y : y + 1, :], corner_in[2 * way, i, pair, y : y + 1, :])
                sides[way, i, pair, end : end + 1] = jnp.where(
                    last, face_in[way, i, pair, rows_x - 1 :, :], corner_in[2 * way + 1, i, pair, y : y + 1, :])


def first_step(cells, tangent, cell_inflow, sens_inflow, w_in, b_in, w_mid, b_mid, w_out, b_out, *rest):
    outs, (cell_state, state), scratch = rest[:6], rest[6:8], rest[8:]
    rows_x, pairs = state.shape[0], state.shape[1]
    cell_state[27 * rows_x :, :] = jnp.zeros((5 * rows_x, LANES), jnp.float32)
    for q in range(27):
        cell_state[q * rows_x : (q + 1) * rows_x, :] = cells[q]

    def load(x, carry):
        for pair in range(pairs):
            for q in range(27):
                state[x, pair, q * 8 : (q + 1) * 8, :] = tangent[q, x, :, pair * LANES : (pair + 1) * LANES]
            state[x, pair, 27 * 8 :, :] = jnp.zeros((5 * 8, LANES), jnp.float32)
        return carry

    lax.fori_loop(0, rows_x, load, 0)
    weights = (w_in, b_in, w_mid, b_mid, w_out, b_out)
    exchange_and_collide(cell_state, state, weights, (cell_inflow, sens_inflow), outs, scratch)


def next_step(z_depth, cells, cell_rows, cell_sides, before, x_rows, sides, cell_inflow, sens_inflow,
              w_in, b_in, w_mid, b_mid, w_out, b_out, *rest):
    outs, (cell_state, state), scratch = rest[:6], rest[6:8], rest[8:]
    rows_x, pairs = state.shape[0], state.shape[1]
    cell_state[27 * rows_x :, :] = jnp.zeros((5 * rows_x, LANES), jnp.float32)

    def keep(q, value):
        cell_state[q * rows_x : (q + 1) * rows_x, :] = value

    primal_stream(cells, cell_rows, cell_sides, keep, z_depth)

    def write(x, q, parts):
        for pair in range(pairs):
            state[x, pair, q * 8 : (q + 1) * 8, :] = parts[pair]
            if q == 0:
                state[x, pair, 27 * 8 :, :] = jnp.zeros((5 * 8, LANES), jnp.float32)

    stream_rows(before, x_rows, sides, write)
    weights = (w_in, b_in, w_mid, b_mid, w_out, b_out)
    exchange_and_collide(cell_state, state, weights, (cell_inflow, sens_inflow), outs, scratch)


def last_step(z_depth, probe_cells, probe_counts, cells, cell_rows, cell_sides, before, x_rows, sides, primal_out, out, rows_out, observed):
    pairs = before.shape[1]
    rows_y = 8
    sums = {}

    def write(x, q, parts):
        vector = LATTICE[q]
        for pair in range(pairs):
            out[q, x, :, pair * LANES : (pair + 1) * LANES] = parts[pair]
            held = sums.setdefault((pair,), [None] * 4) if q else sums.__setitem__((pair,), [None] * 4) or sums[(pair,)]
            for m, factor in enumerate((1,) + vector):
                if factor == 0:
                    continue
                if held[m] is None:
                    held[m] = parts[pair] if factor == 1 else -parts[pair]
                else:
                    held[m] = held[m] + parts[pair] if factor == 1 else held[m] - parts[pair]
            if q == 26:
                for m in range(4):
                    observed[m, pair, pl.ds(pl.multiple_of(x * rows_y, rows_y), rows_y), :] = held[m]

    def keep(q, value):
        primal_out[q] = value

    primal_stream(cells, cell_rows, cell_sides, keep, z_depth)
    stream_rows(before, x_rows, sides, write)
    peers, slots = probe_cells.shape
    left = lane_iota(1) < LANES // 2

    def probe(peer, carry):
        for slot in range(slots):
            cell = jnp.clip(probe_cells[peer, slot], 0, observed.shape[2] * z_depth - 1)
            place, z = cell // z_depth, cell % z_depth
            pair, odd = z // 2, z % 2
            live = slot < probe_counts[0, peer]
            rows = [observed[m, pair, pl.ds(place, 1), :] for m in range(4)]
            turned = [pltpu.roll(r, LANES // 2, 1) for r in rows]
            for m in (0, 2):
                low = jnp.where(odd == 1, turned[m], rows[m])
                high = jnp.where(odd == 1, rows[m + 1], turned[m + 1])
                value = jnp.where(left, low, high)
                rows_out[peer, slot : slot + 1, m * 64 : m * 64 + LANES] = jnp.where(live, value, 0.0)
        return carry

    lax.fori_loop(0, peers, probe, 0, unroll=2)


def shape(*dims):
    return jax.ShapeDtypeStruct(dims, jnp.float32)


def call(body, outs, scratch=(), collective=None, **more):
    params = {} if collective is None else {"collective_id": collective, "has_side_effects": True}
    return pl.pallas_call(
        body,
        out_shape=outs,
        scratch_shapes=list(scratch),
        compiler_params=pltpu.CompilerParams(vmem_limit_bytes=VMEM_LIMIT, **params),
        **more,
    )


def near_inflow(values, row_at, rows_y):
    around = jnp.concatenate([values[:, -rows_y:], values, values[:, :rows_y]], axis=1)
    return lax.dynamic_slice_in_dim(around, row_at, 3 * rows_y, 1).reshape(9, 3, rows_y, -1)


def on_device(primal_pops, tangent_pops, inflow_pops, inflow_sens, w_in, b_in, w_mid, b_mid, w_out, b_out,
              probe_cells, probe_counts):
    rows_x, rows_y, z_depth = primal_pops.shape[1:]
    width = tangent_pops.shape[3]
    pairs = width // LANES
    hidden = w_in.shape[0]
    row_at = lax.axis_index("gy") * rows_y

    w_in = jnp.pad(w_in, ((0, 0), (0, QS - 27)))
    w_out = jnp.pad(w_out, ((0, QS - 27), (0, 0)))
    weights = (w_in, b_in[:, None], w_mid, b_mid[:, None], w_out, jnp.pad(b_out, (0, QS - 27))[:, None])
    tall = ((0, 0), (0, 0), (0, LANES - z_depth * rows_y))
    cells = jnp.pad(jnp.swapaxes(primal_pops, 2, 3).reshape(27, rows_x, z_depth * rows_y), tall)
    inflow = jnp.transpose(near_inflow(inflow_pops, row_at, rows_y), (1, 0, 3, 2)).reshape(3, 9, z_depth * rows_y)
    inflow = jnp.pad(inflow, ((0, 0), (0, 7), (0, LANES - z_depth * rows_y)))
    sens = near_inflow(inflow_sens, row_at, rows_y).reshape(9, 3, rows_y, pairs, LANES)
    sens = jnp.transpose(sens, (1, 0, 3, 2, 4))

    tall_x = rows_x + 8
    outs = (
        shape(27, rows_x, LANES),
        shape(2, 16, LANES),
        shape(2, 9, tall_x, LANES),
        shape(rows_x, pairs, QS * rows_y, LANES),
        shape(2, 9, pairs, rows_y, LANES),
        shape(2, 9, pairs, tall_x, LANES),
    )

    def room(*dims, kind=jnp.float32):
        return pltpu.VMEM(dims, kind)

    scratch = [
        room(QS * rows_x, LANES),
        room(rows_x, pairs, QS * rows_y, LANES),
        room(rows_x, hidden, LANES),
        room(rows_x, hidden, LANES),
        room(hidden, 3 * QS, kind=jnp.bfloat16),
        room(2 * hidden, 2 * hidden, kind=jnp.bfloat16),
        room(2 * QS, 2 * hidden, kind=jnp.bfloat16),
        room(2, 16, LANES),
        room(2, 9, rows_x, LANES),
        room(2, 9, pairs, rows_y, LANES),
        room(2, 9, pairs, rows_x, LANES),
        room(2, 16, LANES),
        room(2, 9, rows_x, LANES),
        room(4, 16, LANES),
        room(2, 9, pairs, rows_y, LANES),
        room(2, 9, pairs, rows_x, LANES),
        room(4, 3, pairs, rows_y, LANES),
        pltpu.SemaphoreType.DMA((16,)),
        pltpu.SemaphoreType.DMA((16,)),
    ]
    held = call(first_step, outs, scratch, 1)(cells, tangent_pops, inflow, sens, *weights)
    for step in range(1, STEPS):
        held = call(functools.partial(next_step, z_depth), outs, scratch, 1 + step)(*held, inflow, sens, *weights)
    peers, slots = probe_cells.shape[1:]
    smem = pl.BlockSpec(memory_space=pltpu.SMEM)
    vmem = pl.BlockSpec(memory_space=pltpu.VMEM)
    primal, tangent, jac = call(
        functools.partial(last_step, z_depth),
        (
            shape(27, rows_x, LANES),
            shape(27, rows_x, rows_y, width),
            shape(peers, slots, 4 * width // z_depth),
        ),
        [room(4, pairs, rows_x * rows_y, LANES)],
        in_specs=[smem, smem] + [vmem] * 6,
    )(probe_cells[0], probe_counts, *held)
    primal = jnp.swapaxes(primal[:, :, : z_depth * rows_y].reshape(27, rows_x, z_depth, rows_y), 2, 3)
    jac = lax.all_to_all(jac[None], ("gx", "gy"), split_axis=1, concat_axis=1, tiled=True)
    return primal, tangent, jac


def solution(mesh):
    both = P(("gx", "gy"))
    split_xy = P(None, "gx", "gy", None)
    return jax.shard_map(
        on_device,
        mesh=mesh,
        in_specs=(split_xy, split_xy) + (P(),) * 8 + (both, both),
        out_specs=(split_xy, split_xy, both),
        check_vma=False,
    )
```

time: 215 us -> 144 us (0.67)
  starting transfers between devices: 42 us -> 7.31 us
  waiting for transfers between devices: 21.5 us -> 5.92 us
  Pallas kernels: 123 us -> 112 us
  other arithmetic: 8.69 us -> 2.58 us
  local copies, waits for them, and re-layouts: 18.2 us -> 15.6 us
    ppermute x16 -> x0, starting transfers between devices: 37.5 us -> none  [the longest x4 15.5 us: edge_rows(): x_low = jnp.where(column == 0, inflow, lax.ppermute(above, 'gx', up))]
    ppermute x16 -> x0, waiting for transfers between devices: 21.5 us -> none  [the longest x4 11.5 us: spread(): lax.ppermute(full(side_high, low_corner[0], high_corner[0]), 'gy', up)]
    pallas_call x6 -> x3, Pallas kernels: 123 us -> 112 us  [the longest x1 51.7 us: on_device(): call(functools.partial(next_step, z_depth), outs, scratch, 1 + step)]
    all_to_all x1, waiting for transfers between devices: 0.01 us -> 5.92 us  [on_device(): lax.all_to_all(jac[None], ('gx', 'gy'), split_axis=1, concat_axis=1, tile...]
    concatenate x10 -> x1, other arithmetic: 5 us -> 0.87 us  [near_inflow(): jnp.concatenate([values[:, -rows_y:], values, values[:, :rows_y]], axis=1)]
    select_n x6 -> x0, other arithmetic: 3.7 us -> none  [the longest x4 1.86 us: edge_rows(): x_low = jnp.where(column == 0, inflow, lax.ppermute(above, 'gx', up))]
    unnamed x42 -> x3, local copies, waits for them, and re-layouts: 4.96 us -> 1.59 us
    all_to_all x1, starting transfers between devices: 4.52 us -> 7.31 us  [on_device(): lax.all_to_all(jac[None], ('gx', 'gy'), split_axis=1, concat_axis=1, tile...]
  transfers between devices with their start and end apart: 17 -> 1, of which waited for: 6 -> 1; matrix products, arithmetic and copies ran while one was open for 6% -> 1% of each run, Pallas kernels for 47% -> 0%
where the time goes in v1:
time: 144 us
  Pallas kernels  112 us (78%)
  local copies, waits for them, and re-layouts  15.6 us (11%)
  starting transfers between devices  7.31 us (5%)
  waiting for transfers between devices  5.92 us (4%)
  other arithmetic  2.58 us (2%)
    pallas_call x1, Pallas kernels, on_device(): call(functools.partial(next_step, z_depth), outs, scratch, 1 + step)  51.7 us
    pallas_call x1, Pallas kernels, on_device(): call(first_step, outs, scratch, 1)  49 us
    pallas_call x1, Pallas kernels, on_device(): call(functools.partial(last_step, z_depth), (shape(27, rows_x, LANES), sh...  10.9 us
    all_to_all x1, starting transfers between devices, on_device(): lax.all_to_all(jac[None], ('gx', 'gy'), split_axis=1, concat_axis=1, tile...  7.31 us
    all_to_all x1, waiting for transfers between devices, on_device(): lax.all_to_all(jac[None], ('gx', 'gy'), split_axis=1, concat_axis=1, tile...  5.92 us
  transfers between devices with their start and end apart: 1, of which 1 were waited for; matrix products, arithmetic and copies ran while one was open for 1% of the time, Pallas kernels for 0%

profile of v1, /device:TPU:0, one launch (start us, length us, event | category | flops | bytes accessed | tf_op | source)
XLA Modules:
  0.0 143.8 jit_solution(5201066336601831888)
XLA Ops:
  0.6 1.0 fusion.3
  1.6 0.9 fusion.4
  2.5 0.9 dynamic-slice_maximum_fusion
  3.4 0.1 copy.59
  3.5 0.2 copy.57
  3.7 0.1 reshape.22
  3.8 0.8 copy.46
  4.7 0.6 pad.21.cell_inflow
  5.3 0.6 pad.22.w_in
  5.9 1.4 copy.47.b_in
  7.3 1.4 copy.48.b_mid
  8.7 0.7 pad_bitcast_fusion
  9.3 0.7 copy.49.b_out
  10.0 1.3 pad.23.w_out
  11.4 1.2 copy.41
  12.6 0.7 pad.20.cells
  13.3 1.4 copy.53.probe_cells
  14.6 1.7 %copy_bitcast_fusion.sens_inflow = f32[3,9,3,8,128]{4,3,2,1,0:T(8,128)} fusion(s32[]{:T(128)S(6)} %select_n.4, f32[9,8,384]{2,1,0:T(8,128)S(1)} %get-tuple-element.37, f32[9,64,384]{2,1,0:T(8,128)} %param.15, f32[9,8,384]{2,1,0:T(8,128)S(1)} %get-tuple-element.36), kind=kLoop, calls=%fused_computation.6 | loop fusion | flops 165888 | bytes 1437700 | tf_op jit(solution)/shard_map/transpose | solution.py:408
  16.3 49.0 %shard_map.139 = (f32[27,16,128]{2,1,0:T(8,128)}, f32[2,16,128]{2,1,0:T(8,128)}, f32[2,9,24,128]{3,2,1,0:T(8,128)}, f32[16,3,256,128]{3,2,1,0:T(8,128)}, f32[2,9...) custom-call(f32[27,16,128]{2,1,0:T(8,128)} %pad.20.cells, f32[27,16,8,384]{3,2,1,0:T(8,128)} %tangent.1, ...), custom_call_target="tpu_custom_call" | custom-call | tf_op jit(solution)/shard_map/pallas_call | solution.py:444
  65.3 51.7 %shard_map.140 = (f32[27,16,128]{2,1,0:T(8,128)}, f32[2,16,128]{2,1,0:T(8,128)}, f32[2,9,24,128]{3,2,1,0:T(8,128)}, f32[16,3,256,128]{3,2,1,0:T(8,128)}, f32[2,9...) custom-call(f32[27,16,128]{2,1,0:T(8,128)} %get-tuple-element.18.cells, f32[2,16,128]{2,1,0:T(8,128)} %get-tuple-element.19.cell_rows, ...), custom_call_target="tpu_custom_call" | custom-call | tf_op jit(solution)/shard_map/pallas_call | solution.py:446
  117.1 10.9 %shard_map.141 = (f32[27,16,128]{2,1,0:T(8,128)}, f32[27,16,8,384]{3,2,1,0:T(8,128)}, f32[32,4,256]{2,1,0:T(4,128)}) custom-call(s32[32,4]{1,0:T(8,128)} %copy.53.probe_cells, s32[1,32]{1,0:T(1,128)} %probe_counts.1, f32[27,16,128]{2,1,0:T(8,128)} %get-tuple-element.24.cells, f32[2,16,128]{2,1,0:T(8,128)} %get-tuple-element.25.cell_rows, ...), custom_call_target="tpu_custom_call" | custom-call | tf_op jit(solution)/shard_map/pallas_call | solution.py:450
  128.0 7.3 %all-to-all-start = ((f32[1,32,4,256]{3,2,0,1:T(4,128)}), f32[1,32,4,256]{3,2,0,1:T(4,128)S(1)}, u32[]{:S(2)}, u32[]{:S(2)}) async-start(f32[1,32,4,256]{3,2,0,1:T(4,128)} %bitcast.29), calls=%async_computation | async-start | bytes 262144 | tf_op jit(solution)/shard_map/all_to_all | solution.py:461
  135.3 1.9 %copy.54 = f32[27,16,48]{0,2,1:T(8,128)} copy(f32[27,16,48]{2,1,0:T(8,128)} %bitcast.28) | data formatting | bytes 165888 | tf_op jit(solution)/shard_map/slice | solution.py:460
  137.2 5.9 %all-to-all-done = f32[1,32,4,256]{3,2,0,1:T(4,128)S(1)} async-done(((f32[1,32,4,256]{3,2,0,1:T(4,128)}), f32[1,32,4,256]{3,2,0,1:T(4,128)S(1)}, u32[]{:S(2)}, u32[]{:S(2)}) %all-to-all-start) | async-done | bytes 131104 | tf_op jit(solution)/shard_map/all_to_all | solution.py:461
  143.1 0.7 copy.62
Async XLA Ops:
  128.0 15.1 %all-to-all-start = ((f32[1,32,4,256]{3,2,0,1:T(4,128)}), f32[1,32,4,256]{3,2,0,1:T(4,128)S(1)}, u32[]{:S(2)}, u32[]{:S(2)}) async-start(f32[1,32,4,256]{3,2,0,1:T(4,128)} %bitcast.29), calls=%async_computation | async-start | bytes 262144 | tf_op jit(solution)/shard_map/all_to_all | solution.py:461

commit v2 on v1

--- a/solution.py
+++ b/solution.py
@@ -30,13 +30,14 @@
 
 
 def make_weights(w_in, w_mid, w_out, one, two, three):
-    high, low = split(w_in[...])
+    hidden = w_mid.shape[0]
+    high, low = split(jnp.concatenate([w_in[...], jnp.zeros((hidden, QS - 27), jnp.float32)], axis=1))
     one[...] = jnp.concatenate([high, high, low], axis=1)
     high, low = split(w_mid[...])
     two[...] = jnp.concatenate(
         [jnp.concatenate([high, high], axis=1), jnp.concatenate([low, jnp.zeros_like(low)], axis=1)], axis=0
     )
-    high, low = split(w_out[...])
+    high, low = split(jnp.concatenate([w_out[...], jnp.zeros((QS - 27, hidden), jnp.float32)], axis=0))
     three[...] = jnp.concatenate(
         [jnp.concatenate([high, high], axis=1), jnp.concatenate([low, jnp.zeros_like(low)], axis=1)], axis=0
     )
@@ -113,22 +114,22 @@
 
 
 def primal_collide(state_ref, biases, post_ref, slope_one_ref, slope_two_ref, one, two, three):
-    b_in, b_mid, b_out = biases
+    bias_in, bias_mid, bias_out = biases
     rows_x = post_ref.shape[1]
     hidden = two.shape[0] // 2
 
     def row(x, carry):
         cell = state_ref[pl.ds(x, QS, stride=rows_x), :]
         high, low = split(cell)
-        act_one = jnp.tanh(dot(one[...], jnp.concatenate([high, low, high], axis=0)) + b_in[...])
+        act_one = jnp.tanh(dot(one[...], jnp.concatenate([high, low, high], axis=0)) + bias_in)
         high, low = split(act_one)
         second = dot(two[...], jnp.concatenate([high, low], axis=0))
-        act_two = jnp.tanh(second[:hidden] + second[hidden:] + b_mid[...])
+        act_two = jnp.tanh(second[:hidden] + second[hidden:] + bias_mid)
         high, low = split(act_two)
         moved = dot(three[...], jnp.concatenate([high, low], axis=0))
         slope_one_ref[x] = 1.0 - act_one * act_one
         slope_two_ref[x] = 1.0 - act_two * act_two
-        state_ref[pl.ds(x, QS, stride=rows_x), :] = cell + moved[:QS] + moved[QS:] + b_out[...]
+        state_ref[pl.ds(x, QS, stride=rows_x), :] = cell + moved[:QS] + moved[QS:] + bias_out
         return carry
 
     lax.fori_loop(0, rows_x, row, 0, unroll=4)
@@ -193,7 +194,12 @@
         copies.append(copy)
 
     make_weights(w_in, w_mid, w_out, one, two, three)
-    primal_collide(cell_state, (b_in, b_mid, b_out), cell_post, slope_one, slope_two, one, two, three)
+    def upright(bias):
+        return jnp.transpose(jnp.broadcast_to(bias, (LANES, LANES)))
+
+    out_bias = jnp.concatenate([b_out[...], jnp.zeros((1, LANES - 27), jnp.float32)], axis=1)
+    biases = (upright(b_in[...]), upright(b_mid[...]), upright(out_bias)[:QS])
+    primal_collide(cell_state, biases, cell_post, slope_one, slope_two, one, two, three)
     cell_edge[0] = cell_state[pl.ds(0, 16, stride=rows_x), :]
     cell_edge[1, :9] = cell_state[pl.ds(18 * rows_x + rows_x - 1, 9, stride=rows_x), :]
     cell_edge[1, 9:] = jnp.zeros((7, LANES), jnp.float32)
@@ -397,9 +403,7 @@
     hidden = w_in.shape[0]
     row_at = lax.axis_index("gy") * rows_y
 
-    w_in = jnp.pad(w_in, ((0, 0), (0, QS - 27)))
-    w_out = jnp.pad(w_out, ((0, QS - 27), (0, 0)))
-    weights = (w_in, b_in[:, None], w_mid, b_mid[:, None], w_out, jnp.pad(b_out, (0, QS - 27))[:, None])
+    weights = (w_in, b_in[None], w_mid, b_mid[None], w_out, b_out[None])
     tall = ((0, 0), (0, 0), (0, LANES - z_depth * rows_y))
     cells = jnp.pad(jnp.swapaxes(primal_pops, 2, 3).reshape(27, rows_x, z_depth * rows_y), tall)
     inflow = jnp.transpose(near_inflow(inflow_pops, row_at, rows_y), (1, 0, 3, 2)).reshape(3, 9, z_depth * rows_y)

time: 144 us -> 139 us (0.965)
  local copies, waits for them, and re-layouts: 15.6 us -> 10.2 us
    broadcast_in_dim x4 -> x0, local copies, waits for them, and re-layouts: 4.13 us -> none  [the longest x1 1.39 us: on_device(): b_mid[:, None]]
    pad x2 -> x0, local copies, waits for them, and re-layouts: 1.95 us -> none  [the longest x1 1.32 us: on_device(): w_out = jnp.pad(w_out, ((0, QS - 27), (0, 0)))]
where the time goes in v2:
time: 139 us; the launch traced here: 138 us
  Pallas kernels  112 us (81%)
  local copies, waits for them, and re-layouts  10.2 us (7%)
  starting transfers between devices  7.32 us (5%)
  waiting for transfers between devices  5.92 us (4%)
  other arithmetic  2.58 us (2%)
    pallas_call x1, Pallas kernels, on_device(): call(functools.partial(next_step, z_depth), outs, scratch, 1 + step)  51.7 us
    pallas_call x1, Pallas kernels, on_device(): call(first_step, outs, scratch, 1)  48.9 us
    pallas_call x1, Pallas kernels, on_device(): call(functools.partial(last_step, z_depth), (shape(27, rows_x, LANES), sh...  10.9 us
    all_to_all x1, starting transfers between devices, on_device(): lax.all_to_all(jac[None], ('gx', 'gy'), split_axis=1, concat_axis=1, tile...  7.32 us
    all_to_all x1, waiting for transfers between devices, on_device(): lax.all_to_all(jac[None], ('gx', 'gy'), split_axis=1, concat_axis=1, tile...  5.92 us
  transfers between devices with their start and end apart: 1, of which 1 were waited for; matrix products, arithmetic and copies ran while one was open for 1% of the time, Pallas kernels for 0%

profile of v2, /device:TPU:0, one launch (start us, length us, event | category | flops | bytes accessed | tf_op | source)
XLA Modules:
  0.0 138.3 jit_solution(16819750827698848435)
XLA Ops:
  0.6 1.0 fusion.3
  1.6 0.9 fusion.4
  2.5 0.9 dynamic-slice_maximum_fusion
  3.4 0.1 copy.44
  3.5 0.2 copy.42
  3.7 0.1 reshape.22
  3.8 1.4 %copy.36.w_in = f32[128,27]{1,0:T(8,128)} copy(f32[128,27]{0,1:T(8,128)} %param.16) | data formatting | bytes 27648 | tf_op args[4]
  5.3 1.2 copy.31
  6.5 0.6 pad.9.cell_inflow
  7.1 0.7 pad.8.cells
  7.8 1.4 copy.38.probe_cells
  9.2 1.7 %copy_bitcast_fusion.sens_inflow = f32[3,9,3,8,128]{4,3,2,1,0:T(8,128)} fusion(s32[]{:T(128)S(6)} %select_n.4, f32[9,8,384]{2,1,0:T(8,128)S(1)} %get-tuple-element.37, f32[9,64,384]{2,1,0:T(8,128)} %param.15, f32[9,8,384]{2,1,0:T(8,128)S(1)} %get-tuple-element.36), kind=kLoop, calls=%fused_computation.6 | loop fusion | flops 165888 | bytes 1437700 | tf_op jit(solution)/shard_map/transpose | solution.py:412
  10.9 48.9 %shard_map.139 = (f32[27,16,128]{2,1,0:T(8,128)}, f32[2,16,128]{2,1,0:T(8,128)}, f32[2,9,24,128]{3,2,1,0:T(8,128)}, f32[16,3,256,128]{3,2,1,0:T(8,128)}, f32[2,9...) custom-call(f32[27,16,128]{2,1,0:T(8,128)} %pad.8.cells, f32[27,16,8,384]{3,2,1,0:T(8,128)} %tangent.1, ...), custom_call_target="tpu_custom_call" | custom-call | tf_op jit(solution)/shard_map/pallas_call | solution.py:448
  59.8 51.7 %shard_map.140 = (f32[27,16,128]{2,1,0:T(8,128)}, f32[2,16,128]{2,1,0:T(8,128)}, f32[2,9,24,128]{3,2,1,0:T(8,128)}, f32[16,3,256,128]{3,2,1,0:T(8,128)}, f32[2,9...) custom-call(f32[27,16,128]{2,1,0:T(8,128)} %get-tuple-element.18.cells, f32[2,16,128]{2,1,0:T(8,128)} %get-tuple-element.19.cell_rows, ...), custom_call_target="tpu_custom_call" | custom-call | tf_op jit(solution)/shard_map/pallas_call | solution.py:450
  111.6 10.9 %shard_map.141 = (f32[27,16,128]{2,1,0:T(8,128)}, f32[27,16,8,384]{3,2,1,0:T(8,128)}, f32[32,4,256]{2,1,0:T(4,128)}) custom-call(s32[32,4]{1,0:T(8,128)} %copy.38.probe_cells, s32[1,32]{1,0:T(1,128)} %probe_counts.1, f32[27,16,128]{2,1,0:T(8,128)} %get-tuple-element.24.cells, f32[2,16,128]{2,1,0:T(8,128)} %get-tuple-element.25.cell_rows, ...), custom_call_target="tpu_custom_call" | custom-call | tf_op jit(solution)/shard_map/pallas_call | solution.py:454
  122.5 7.3 %all-to-all-start = ((f32[1,32,4,256]{3,2,0,1:T(4,128)}), f32[1,32,4,256]{3,2,0,1:T(4,128)S(1)}, u32[]{:S(2)}, u32[]{:S(2)}) async-start(f32[1,32,4,256]{3,2,0,1:T(4,128)} %bitcast.28), calls=%async_computation | async-start | bytes 262144 | tf_op jit(solution)/shard_map/all_to_all | solution.py:465
  129.8 1.9 %copy.39 = f32[27,16,48]{0,2,1:T(8,128)} copy(f32[27,16,48]{2,1,0:T(8,128)} %bitcast.27) | data formatting | bytes 165888 | tf_op jit(solution)/shard_map/slice | solution.py:464
  131.7 5.9 %all-to-all-done = f32[1,32,4,256]{3,2,0,1:T(4,128)S(1)} async-done(((f32[1,32,4,256]{3,2,0,1:T(4,128)}), f32[1,32,4,256]{3,2,0,1:T(4,128)S(1)}, u32[]{:S(2)}, u32[]{:S(2)}) %all-to-all-start) | async-done | bytes 131104 | tf_op jit(solution)/shard_map/all_to_all | solution.py:465
  137.6 0.7 copy.47
Async XLA Ops:
  122.5 15.1 %all-to-all-start = ((f32[1,32,4,256]{3,2,0,1:T(4,128)}), f32[1,32,4,256]{3,2,0,1:T(4,128)S(1)}, u32[]{:S(2)}, u32[]{:S(2)}) async-start(f32[1,32,4,256]{3,2,0,1:T(4,128)} %bitcast.28), calls=%async_computation | async-start | bytes 262144 | tf_op jit(solution)/shard_map/all_to_all | solution.py:465
